TPU v7x, 32 devices: a whole 2x2x4 slice. The times are simulated.
32 devices in a mesh: snp: 8 (over z, x), trait: 4 (over y, core).
Axes of the slice: x: 2, y: 2, z: 4, core: 2. Of those that a mesh axis runs over, the one named last changes fastest.
Arguments:
- genotype: bfloat16 [32, 8192], P(None, 'snp'), may hold values from -0.0625 to 0.0625
- targets: bfloat16 [32, 16384], P('snp', 'trait'), may hold values from -6 to 6
- effect_sizes: float32 [8192, 16384], P('snp', 'trait'), may hold values from -6 to 6
- membership: int32 [4, 128, 128], replicated, may hold values from 0 to 1, as said below
- node_weight: float32 [4, 128], replicated, may hold values from 0.03 to 1
Outputs:
- updated: float32 [8192, 16384], P('snp', 'trait')
Inputs may be any that keep to these rules, and one draw needn't show every extreme that they name: `membership`: at each level the node slots 0 .. c - 1 partition all 128 trait blocks, the remaining slots cover none; every node of a level lies inside one node of the next level; at level 0 each block is its own node.
All inputs are finite; a program needn't handle non-finite values.
Results may differ from a plain program's by a relative error of at most 0.00042.
Values may be sent and summed in bfloat16 or wider, within the bound.
A program may use at most 128 MiB of HBM per device.

v0:
```python
import jax
import jax.numpy as jnp
from jax import lax
from jax.sharding import PartitionSpec as P

TB = 128
LEVELS = 4


step_size = 0.5


def factor_of(node_sq, threshold):
    norm = jnp.sqrt(node_sq)
    return jnp.maximum(norm - threshold, 0.0) / jnp.maximum(norm, threshold)


def shrink_local(value, membership, node_weight):
    local_blocks = value.shape[1] // TB
    first_block = lax.axis_index("trait") * local_blocks
    for level in range(LEVELS):
        member_all = membership[level].astype(jnp.float32)
        count = jnp.sum(member_all, axis=1)
        threshold = step_size * node_weight[level] * jnp.sqrt(TB * jnp.maximum(count, 1.0))
        member = lax.dynamic_slice_in_dim(member_all, first_block, local_blocks, 1)
        blocks = value.reshape(value.shape[0], local_blocks, TB)
        block_sq = jnp.sum(blocks * blocks, axis=2)
        partial_sq = jnp.dot(block_sq, member.T, precision=lax.Precision.HIGHEST)
        node_sq = lax.psum(partial_sq, "trait")
        factor = factor_of(node_sq, threshold)
        block_factor = jnp.dot(factor, member, precision=lax.Precision.HIGHEST)
        value = (blocks * block_factor[:, :, None]).reshape(value.shape)
    return value


def body(genotype, targets, effect_sizes, membership, node_weight):
    current = effect_sizes
    targets_full = lax.all_gather(targets, "snp", axis=0, tiled=True)
    current_bf = current.astype(jnp.bfloat16)
    fitted = lax.psum(jnp.dot(genotype, current_bf, preferred_element_type=jnp.float32), "snp")
    residual = (targets_full.astype(jnp.float32) - fitted).astype(jnp.bfloat16)
    gradient = lax.dot_general(
        genotype, residual, (((0,), (0,)), ((), ())), preferred_element_type=jnp.float32
    )
    current = shrink_local(current + step_size * gradient, membership, node_weight)
    return current


def solution(mesh):
    return jax.shard_map(
        body,
        mesh=mesh,
        in_specs=(P(None, "snp"), P("snp", "trait"), P("snp", "trait"), P(), P()),
        out_specs=P("snp", "trait"),
        check_vma=False,
    )
```

profile of v0, /device:TPU:0, one launch (start us, length us, event | category | flops | bytes accessed | tf_op | source)
XLA Modules:
  0.0 313.8 jit_solution(9431012328404320103)
XLA Ops:
  6.5 0.0 copy-start
  6.5 0.0 all-reduce.6.cloned.1.call-start
  6.5 0.8 copy-done
  7.4 8.1 %fusion = f32[32,4096]{1,0:T(8,128)} fusion(bf16[32,1024]{1,0:T(8,128)(2,1)S(1)} %copy-done, f32[1024,4096]{1,0:T(8,128)} %param.7), kind=kOutput, calls=%fused_computation.9 | convolution fusion | flops 272629760 | bytes 17367040 | tf_op jit(solution)/shard_map/dot_general | solution.py:40
  15.5 0.0 all-reduce.6.cloned.1.call-update
  15.5 0.0 all-reduce.8.cloned.1.call-start
  15.6 0.0 copy-start.3
  15.6 0.0 copy-start.2
  15.6 17.5 %copy.8 = f32[1024,4096]{0,1:T(8,128)} copy(f32[1024,4096]{1,0:T(8,128)} %param.7) | data formatting | bytes 33554432 | tf_op args[2]
  33.1 0.0 copy-done.3
  33.1 32.6 %all-gather = bf16[8,4,4096]{2,1,0:T(4,128)(2,1)S(1)} all-gather(bf16[1,4,4096]{2,1,0:T(4,128)(2,1)S(1)} %bitcast.72), channel_id=1, replica_groups=mesh['snp'=8,'trait'=4] {'snp'}, dimensions={0}, use_global_device_ids=true | all-gather | bytes 294912 | tf_op jit(solution)/shard_map/all_gather | solution.py:38
  65.8 0.0 copy-done.2
  65.8 0.0 copy-start.4
  65.8 25.0 %all-reduce.6.cloned.1.call-done = f32[32,4096]{1,0:T(8,128)} async-done(((f32[32,4096]{1,0:T(8,128)}), f32[32,4096]{1,0:T(8,128)}) %all-reduce.6.cloned.1.call-update) | async-done | bytes 524304 | tf_op jit(solution)/shard_map/psum | solution.py:40
  90.8 11.0 %multiply_reduce_fusion.3 = (f32[1024,32]{0,1:T(8,128)S(1)}, f32[1024,4096]{0,1:T(8,128)}) fusion(f32[1024,4096]{0,1:T(8,128)} %copy.8, bf16[32,1024]{1,0:T(8,128)(2,1)S(1)} %copy-done, f32[32,4096]{1,0:T(8,128)S(1)} %reshape.95, f32[32,4096]{1,0:T(8,128)} %all-reduce.6.cloned.1.call-done), kind=kOutput, calls=%fused_computation.8 | convolution fusion | flops 285442048 | bytes 34799616 | tf_op jit(solution)/shard_map/dot_general | solution.py:42
  101.8 1.8 fusion.24
  103.7 0.0 all-reduce.8.cloned.1.call-update
  103.7 0.0 all-reduce.10.cloned.1.call-start
  103.8 0.1 fusion.53
  103.9 0.0 copy-done.4
  103.9 32.4 %all-reduce.8.cloned.1.call-done = f32[1024,128]{1,0:T(8,128)} async-done(((f32[1024,128]{1,0:T(8,128)}), f32[1024,128]{1,0:T(8,128)}) %all-reduce.8.cloned.1.call-update) | async-done | bytes 524304 | tf_op jit(solution)/shard_map/psum | solution.py:29
  136.3 1.8 fusion.2
  138.2 8.5 %multiply_reduce_fusion.2 = f32[1024,32]{0,1:T(8,128)S(1)} fusion(f32[1024,4096]{0,1:T(8,128)} %get-tuple-element.18, f32[1024,32]{0,1:T(8,128)S(1)} %fusion.2), kind=kLoop, calls=%fused_computation.7 | loop fusion | flops 12550144 | bytes 17039360 | tf_op jit(solution)/shard_map/reduce_sum | solution.py:27
  146.7 1.9 fusion.21
  148.5 0.0 all-reduce.10.cloned.1.call-update
  148.6 0.2 all-reduce.12.cloned.1.call-start
  148.8 33.1 %all-reduce.10.cloned.1.call-done = f32[1024,128]{1,0:T(8,128)} async-done(((f32[1024,128]{1,0:T(8,128)}), f32[1024,128]{1,0:T(8,128)}) %all-reduce.10.cloned.1.call-update) | async-done | bytes 524304 | tf_op jit(solution)/shard_map/psum | solution.py:29
  181.9 1.8 fusion.3
  183.7 9.5 %multiply_reduce_fusion.1 = f32[1024,32]{0,1:T(8,128)S(1)} fusion(f32[1024,4096]{0,1:T(8,128)} %get-tuple-element.18, f32[1024,32]{0,1:T(8,128)S(1)} %fusion.3, f32[1024,32]{0,1:T(8,128)S(1)} %fusion.2), kind=kLoop, calls=%fused_computation.6 | loop fusion | flops 16744448 | bytes 17170432 | tf_op jit(solution)/shard_map/reduce_sum | solution.py:27
  193.2 1.9 fusion.18
  195.1 0.0 all-reduce.12.cloned.1.call-update
  195.1 0.3 all-reduce.14.cloned.1.call-start
  195.4 33.1 %all-reduce.12.cloned.1.call-done = f32[1024,128]{1,0:T(8,128)} async-done(((f32[1024,128]{1,0:T(8,128)}), f32[1024,128]{1,0:T(8,128)}) %all-reduce.12.cloned.1.call-update) | async-done | bytes 524304 | tf_op jit(solution)/shard_map/psum | solution.py:29
  228.4 1.8 fusion.4
  230.2 10.6 %multiply_reduce_fusion = f32[1024,32]{0,1:T(8,128)S(1)} fusion(f32[1024,4096]{0,1:T(8,128)} %get-tuple-element.18, f32[1024,32]{0,1:T(8,128)S(1)} %fusion.4, f32[1024,32]{0,1:T(8,128)S(1)} %fusion.3, f32[1024,32]{0,1:T(8,128)S(1)} %fusion.2), kind=kLoop, calls=%fused_computation.5 | loop fusion | flops 20938752 | bytes 17301504 | tf_op jit(solution)/shard_map/reduce_sum | solution.py:27
  240.8 1.9 fusion.15
  242.7 0.0 all-reduce.14.cloned.1.call-update
  242.7 33.3 %all-reduce.14.cloned.1.call-done = f32[1024,128]{1,0:T(8,128)} async-done(((f32[1024,128]{1,0:T(8,128)}), f32[1024,128]{1,0:T(8,128)}) %all-reduce.14.cloned.1.call-update) | async-done | bytes 524304 | tf_op jit(solution)/shard_map/psum | solution.py:29
  276.0 1.8 fusion.5
  277.9 0.0 copy-start.1
  277.9 12.0 %bitcast_multiply_fusion = f32[1024,4096]{0,1:T(8,128)} fusion(f32[1024,4096]{0,1:T(8,128)} %get-tuple-element.18, f32[1024,32]{0,1:T(8,128)S(1)} %fusion.5, f32[1024,32]{0,1:T(8,128)S(1)} %fusion.4, f32[1024,32]{0,1:T(8,128)S(1)} %fusion.3, f32[1024,32]{0,1:T(8,128)S(1)} %fusion.2), kind=kLoop, calls=%fused_computation | loop fusion | flops 16777216 | bytes 34078720 | tf_op jit(solution)/shard_map/mul | solution.py:32
  289.9 17.4 %copy.9 = f32[1024,4096]{1,0:T(8,128)} copy(f32[1024,4096]{0,1:T(8,128)} %bitcast_multiply_fusion) | data formatting | bytes 33554432 | tf_op jit(solution)/shard_map/mul | solution.py:32
  307.3 0.0 copy-done.1
  (3 shorter events, 0.1 us)
Async XLA Ops:
  6.5 0.8 copy-start
  6.5 84.3 %all-reduce.6.cloned.1.call-start = ((), (), s32[]{:S(2)}) async-start(), calls=%async_computation | async-start | bytes 1048576 | tf_op jit(solution)/shard_map/psum | solution.py:40
  15.5 120.8 %all-reduce.8.cloned.1.call-start = ((), (), s32[]{:S(2)}) async-start(), calls=%async_computation.1 | async-start | bytes 1048576 | tf_op jit(solution)/shard_map/psum | solution.py:29
  15.6 17.5 %copy-start.3 = (bf16[4,4096]{1,0:T(4,128)(2,1)S(1)}, bf16[4,4096]{1,0:T(4,128)(2,1)}, u32[]{:S(2)}) copy-start(bf16[4,4096]{1,0:T(4,128)(2,1)} %param.6) | copy-start | bytes 98308
  15.6 50.2 %copy-start.2 = (s32[4,128,128]{2,1,0:T(8,128)S(1)}, s32[4,128,128]{2,1,0:T(8,128)}, u32[]{:S(2)}) copy-start(s32[4,128,128]{2,1,0:T(8,128)} %param.8) | copy-start | bytes 786436
  65.8 38.1 %copy-start.4 = (f32[4,128]{1,0:T(4,128)S(1)}, f32[4,128]{1,0:T(4,128)}, u32[]{:S(2)}) copy-start(f32[4,128]{1,0:T(4,128)} %param.9) | copy-start | bytes 6148
  103.7 78.2 %all-reduce.10.cloned.1.call-start = ((), (), s32[]{:S(2)}) async-start(), calls=%async_computation.2 | async-start | bytes 1048576 | tf_op jit(solution)/shard_map/psum | solution.py:29
  148.6 79.8 %all-reduce.12.cloned.1.call-start = ((), (), s32[]{:S(2)}) async-start(), calls=%async_computation.3 | async-start | bytes 1048576 | tf_op jit(solution)/shard_map/psum | solution.py:29
  195.1 80.9 %all-reduce.14.cloned.1.call-start = ((), (), s32[]{:S(2)}) async-start(), calls=%async_computation.4 | async-start | bytes 1048576 | tf_op jit(solution)/shard_map/psum | solution.py:29
  277.9 29.4 %copy-start.1 = (bf16[32,1024]{1,0:T(8,128)(2,1)S(1)}, bf16[32,1024]{1,0:T(8,128)(2,1)}, u32[]{:S(2)}) copy-start(bf16[32,1024]{1,0:T(8,128)(2,1)} %param.5) | copy-start | bytes 196612
Sparse Core Ops, SparseCore 0:
  15.6 75.1 all-reduce.5
  103.8 32.4 all-reduce.7
  148.7 33.1 all-reduce.9
  195.2 33.1 all-reduce.11
  242.8 33.1 all-reduce.13
where the time goes:
time: 315 us; the launch traced here: 314 us
  waiting for transfers between devices  157 us (50%)
  other arithmetic  40.7 us (13%)
  local copies, waits for them, and re-layouts  35.8 us (11%)
  matrix products  33.9 us (11%)
  blocking collectives  32.6 us (10%)
  between operations  13.3 us (4%)
    psum x4, waiting for transfers between devices, shrink_local(): node_sq = lax.psum(partial_sq, 'trait')  132 us
    all_gather x1, blocking collectives, body(): targets_full = lax.all_gather(targets, 'snp', axis=0, tiled=True)  32.6 us
    reduce_sum x3, other arithmetic, shrink_local(): block_sq = jnp.sum(blocks * blocks, axis=2)  28.6 us
    psum x1, waiting for transfers between devices, body(): lax.psum(jnp.dot(genotype, current_bf, preferred_element_type=jnp.float32...  25 us
    unnamed x11, local copies, waits for them, and re-layouts  18.4 us
    mul x1, local copies, waits for them, and re-layouts, shrink_local(): value = (blocks * block_factor[:, :, None]).reshape(value.shape)  17.4 us
    mul x1, other arithmetic, shrink_local(): value = (blocks * block_factor[:, :, None]).reshape(value.shape)  12 us
    dot_general x1, matrix products, body(): lax.dot_general(genotype, residual, (((0,), (0,)), ((), ())), preferred_e...  11 us
  transfers between devices with their start and end apart: 5, of which 5 were waited for; matrix products, arithmetic and copies ran while one was open for 6% of the time, Pallas kernels for 0%

commit v1 on v0

v1 whole, which is shorter than its diff:
```python
import functools

import jax
import jax.numpy as jnp
from jax import lax
from jax.experimental import pallas as pl
from jax.experimental.pallas import tpu as pltpu
from jax.sharding import PartitionSpec as P

TB = 128
SUB = 8
STEP = 0.5
F32 = jnp.float32
BF16 = jnp.bfloat16
WIRE = jnp.float32
MESH = pl.DeviceIdType.MESH
HIGH = lax.Precision.HIGHEST
NT = (((1,), (1,)), ((), ()))
TN = (((0,), (0,)), ((), ()))


def one_hot_rows(rows, samples, per, half):
    r = lax.broadcasted_iota(jnp.int32, (rows, samples), 0)
    n = lax.broadcasted_iota(jnp.int32, (rows, samples), 1)
    owner = lax.shift_right_logical(r, 3)
    inner = jnp.bitwise_and(r, 7) - half * per
    hit = (n == owner * per + inner) & (inner >= 0) & (inner < per)
    return jnp.where(hit, 1.0, 0.0).astype(BF16)


def fit_kernel(
    n, trait, chunks, row_tile,
    g_ref, t_ref, m_ref, w_ref, e_hbm,
    v_ref, sc_ref,
    send, got, res, rg, gs, gt, bq, bt, gq, so, si, ssum, thr,
    e_sem, rs_send, rs_recv, ag_send, ag_recv, x_send, x_recv, y_send, y_recv,
):
    me = lax.axis_index("snp")
    mt = lax.axis_index("trait")
    samples, rows = g_ref.shape
    per = samples // n
    halves = SUB // per
    cols = v_ref.shape[1]
    half = cols // halves
    w = half // chunks
    blocks = cols // TB
    levels = m_ref.shape[0]
    q = rows // trait

    def col(h, c):
        return pl.ds(pl.multiple_of(h * half + c * w, w), w)

    def part(c):
        return pl.ds(pl.multiple_of(c * w, w), w)

    def load(h, c):
        return pltpu.make_async_copy(
            e_hbm.at[:, col(h, c)], v_ref.at[:, col(h, c)], e_sem.at[c, h]
        )

    for c in range(chunks):
        for h in range(halves):
            load(h, c).start()

    barrier = pltpu.get_barrier_semaphore()

    def greet_snp(k, _):
        pl.semaphore_signal(
            barrier, inc=1, device_id={"snp": lax.rem(me + k, n)}, device_id_type=MESH
        )
        return 0

    def greet_trait(k, _):
        pl.semaphore_signal(
            barrier, inc=1, device_id={"trait": lax.rem(mt + k, trait)}, device_id_type=MESH
        )
        return 0

    lax.fori_loop(1, n, greet_snp, 0)
    lax.fori_loop(1, trait, greet_trait, 0)

    for h in range(halves):
        pick = one_hot_rows(n * SUB, samples, per, h)
        gs[h] = jnp.dot(pick, g_ref[...], preferred_element_type=F32).astype(BF16)
        gt[h] = lax.dot_general(
            g_ref[...], pick, (((0,), (1,)), ((), ())), preferred_element_type=F32
        ).astype(BF16)

    pl.semaphore_wait(barrier, n + trait - 2)

    def rs_copy(c, to, frm):
        return pltpu.make_async_remote_copy(
            src_ref=send.at[to, :, part(c)],
            dst_ref=got.at[frm, :, part(c)],
            send_sem=rs_send.at[c, to],
            recv_sem=rs_recv.at[c, frm],
            device_id={"snp": to},
            device_id_type=MESH,
        )

    def ag_copy(c, to, frm):
        return pltpu.make_async_remote_copy(
            src_ref=res.at[:, part(c)],
            dst_ref=rg.at[frm, :, part(c)],
            send_sem=ag_send.at[c, to],
            recv_sem=ag_recv.at[c, frm],
            device_id={"snp": to},
            device_id_type=MESH,
        )

    def x_copy(to, frm):
        return pltpu.make_async_remote_copy(
            src_ref=bt.at[to],
            dst_ref=gq.at[frm],
            send_sem=x_send.at[to],
            recv_sem=x_recv.at[frm],
            device_id={"trait": to},
            device_id_type=MESH,
        )

    def y_copy(to, frm):
        return pltpu.make_async_remote_copy(
            src_ref=so.at[to],
            dst_ref=si.at[frm],
            send_sem=y_send.at[to],
            recv_sem=y_recv.at[frm],
            device_id={"trait": to},
            device_id_type=MESH,
        )

    def peers(count, own, fn):
        def step(k, _):
            fn(lax.rem(own + k, count))
            return 0

        lax.fori_loop(1, count, step, 0)

    kt = min(rows, 256)

    def fit_chunk(c, _):
        total = jnp.zeros((n * SUB, w), F32)
        for h in range(halves):
            load(h, c).wait()
            for k in range(rows // kt):
                total += jnp.dot(
                    gs[h, :, k * kt : (k + 1) * kt],
                    v_ref[k * kt : (k + 1) * kt, col(h, c)].astype(BF16),
                    preferred_element_type=F32,
                )
        send[:, :, part(c)] = total.reshape(n, SUB, w).astype(send.dtype)
        got[me, :, part(c)] = send[me, :, part(c)]
        peers(n, me, lambda p: rs_copy(c, p, me).start())
        return 0

    lax.fori_loop(0, chunks, fit_chunk, 0)

    for level in range(levels):
        member = m_ref[level].astype(F32)
        count = jnp.sum(member, axis=1, keepdims=True)
        weight = jnp.broadcast_to(w_ref[level : level + 1, :], member.shape).T
        by_node = STEP * weight * jnp.sqrt(TB * jnp.maximum(count, 1.0))
        thr[level] = lax.dot_general(
            member, by_node, TN, precision=HIGH, preferred_element_type=F32
        )
        ssum[level] = lax.dot_general(
            member, member, TN, precision=HIGH, preferred_element_type=F32
        )

    def res_chunk(c, _):
        peers(n, me, lambda p: rs_copy(c, p, p).wait_recv())
        fitted = jnp.sum(got[:, :, part(c)].astype(F32), axis=0)
        target = jnp.concatenate(
            [t_ref[:, col(h, c)].astype(F32) for h in range(halves)], axis=0
        )
        residual = (target - fitted).astype(BF16)
        res[:, part(c)] = residual
        rg[me, :, part(c)] = residual
        peers(n, me, lambda p: ag_copy(c, p, me).start())
        return 0

    lax.fori_loop(0, chunks, res_chunk, 0)

    lane = lax.broadcasted_iota(jnp.int32, (row_tile, TB), 1)

    def value_chunk(c, _):
        peers(n, me, lambda p: ag_copy(c, p, p).wait_recv())
        resid = rg[:, :, part(c)].reshape(n * SUB, w)

        def tile(i, _):
            r = pl.ds(pl.multiple_of(i * row_tile, row_tile), row_tile)
            sums = bq[r, :]
            for h in range(halves):
                grad = jnp.dot(gt[h, r, :], resid, preferred_element_type=F32)
                value = v_ref[r, col(h, c)] + STEP * grad
                v_ref[r, col(h, c)] = value
                sq = value * value
                first = (h * half + c * w) // TB
                for b in range(w // TB):
                    s = jnp.sum(sq[:, b * TB : (b + 1) * TB], axis=1, keepdims=True)
                    sums = jnp.where(lane == first + b, s, sums)
            bq[r, :] = sums
            return 0

        lax.fori_loop(0, rows // row_tile, tile, 0)
        return 0

    bq[...] = jnp.zeros_like(bq)
    lax.fori_loop(0, chunks, value_chunk, 0)

    for k in range(trait):
        bt[k] = bq[k * q : (k + 1) * q, :].T[:blocks]
    peers(trait, mt, lambda p: x_copy(p, mt).start())
    gq[mt] = bt[mt]
    peers(trait, mt, lambda p: x_copy(p, p).wait_recv())

    block_sq = gq[...].reshape(trait * blocks, q)
    scale = None
    for level in range(levels):
        if level == 0:
            node_sq = block_sq
        else:
            node_sq = jnp.dot(
                ssum[level], block_sq, precision=HIGH, preferred_element_type=F32
            )
        norm = jnp.sqrt(node_sq)
        limit = thr[level][:, :1]
        factor = jnp.maximum(norm - limit, 0.0) / jnp.maximum(norm, limit)
        scale = factor if scale is None else scale * factor
        block_sq = block_sq * (factor * factor)
    so[...] = scale.reshape(trait, blocks, q)
    peers(trait, mt, lambda p: y_copy(p, mt).start())
    si[mt] = so[mt]
    peers(trait, mt, lambda p: y_copy(p, p).wait_recv())
    for k in range(trait):
        sc_ref[k * q : (k + 1) * q, :blocks] = si[k].T

    def drain(c, _):
        peers(n, me, lambda p: rs_copy(c, p, me).wait_send())
        peers(n, me, lambda p: ag_copy(c, p, me).wait_send())
        return 0

    lax.fori_loop(0, chunks, drain, 0)
    peers(trait, mt, lambda p: x_copy(p, mt).wait_send())
    peers(trait, mt, lambda p: y_copy(p, mt).wait_send())


def scale_kernel(pieces, row_tile, v_ref, sc_ref, o_hbm, out, sem):
    rows, cols = v_ref.shape
    size = rows // pieces

    def store(p):
        r = pl.ds(pl.multiple_of(p * size, size), size)
        return pltpu.make_async_copy(out.at[r, :], o_hbm.at[r, :], sem.at[p])

    def piece(p, _):
        def tile(i, _):
            start = pl.multiple_of(p * size + i * row_tile, row_tile)
            r = pl.ds(start, row_tile)
            sc = sc_ref[r, :]
            for b in range(cols // TB):
                c = slice(b * TB, (b + 1) * TB)
                out[r, c] = v_ref[r, c] * sc[:, b : b + 1]
            return 0

        lax.fori_loop(0, size // row_tile, tile, 0)
        store(p).start()
        return 0

    lax.fori_loop(0, pieces, piece, 0)
    lax.fori_loop(0, pieces, lambda p, _: (store(p).wait(), 0)[1], 0)


def body(n, trait, genotype, targets, effect_sizes, membership, node_weight):
    samples, rows = genotype.shape
    cols = effect_sizes.shape[1]
    blocks = cols // TB
    levels, nodes, _ = membership.shape
    halves = SUB // (samples // n)
    half = cols // halves
    chunks = 4
    q = rows // trait
    vmem = pl.BlockSpec(memory_space=pltpu.VMEM)
    hbm = pl.BlockSpec(memory_space=pl.ANY)
    dma = pltpu.SemaphoreType.DMA
    value, scale = pl.pallas_call(
        functools.partial(fit_kernel, n, trait, chunks, min(rows, 64)),
        name="fit",
        out_shape=(pltpu.VMEM((rows, cols), F32), pltpu.VMEM((rows, TB), F32)),
        in_specs=[vmem] * 4 + [hbm],
        out_specs=(vmem, vmem),
        scratch_shapes=[
            pltpu.VMEM((n, SUB, half), WIRE),
            pltpu.VMEM((n, SUB, half), WIRE),
            pltpu.VMEM((SUB, half), BF16),
            pltpu.VMEM((n, SUB, half), BF16),
            pltpu.VMEM((halves, n * SUB, rows), BF16),
            pltpu.VMEM((halves, rows, n * SUB), BF16),
            pltpu.VMEM((rows, TB), F32),
            pltpu.VMEM((trait, blocks, q), F32),
            pltpu.VMEM((trait, blocks, q), F32),
            pltpu.VMEM((trait, blocks, q), F32),
            pltpu.VMEM((trait, blocks, q), F32),
            pltpu.VMEM((levels, nodes, nodes), F32),
            pltpu.VMEM((levels, nodes, nodes), F32),
            dma((chunks, halves)),
            dma((chunks, n)),
            dma((chunks, n)),
            dma((chunks, n)),
            dma((chunks, n)),
            dma((trait,)),
            dma((trait,)),
            dma((trait,)),
            dma((trait,)),
        ],
        compiler_params=pltpu.CompilerParams(
            collective_id=0, has_side_effects=True, vmem_limit_bytes=40 << 20
        ),
    )(genotype, targets, membership, node_weight, effect_sizes)
    pieces = 8
    return pl.pallas_call(
        functools.partial(scale_kernel, pieces, min(rows // pieces, 32)),
        name="scale",
        out_shape=jax.ShapeDtypeStruct((rows, cols), F32),
        in_specs=[vmem, vmem],
        out_specs=hbm,
        scratch_shapes=[pltpu.VMEM((rows, cols), F32), dma((pieces,))],
        compiler_params=pltpu.CompilerParams(vmem_limit_bytes=40 << 20),
    )(value, scale)


def solution(mesh):
    n, trait = mesh.shape["snp"], mesh.shape["trait"]
    return jax.shard_map(
        functools.partial(body, n, trait),
        mesh=mesh,
        in_specs=(P(None, "snp"), P("snp", "trait"), P("snp", "trait"), P(), P()),
        out_specs=P("snp", "trait"),
        check_vma=False,
    )
```

time: 315 us -> 71.6 us (0.23)
  waiting for transfers between devices: 157 us -> 0 us
  Pallas kernels: 0 us -> 65.7 us
  other arithmetic: 40.7 us -> 0 us
  matrix products: 33.9 us -> 0 us
  blocking collectives: 32.6 us -> 0 us
  local copies, waits for them, and re-layouts: 35.8 us -> 5.71 us
  between operations: 13.3 us -> 0.02 us
    psum x5 -> x0, waiting for transfers between devices: 157 us -> none  [the longest x4 132 us: shrink_local(): node_sq = lax.psum(partial_sq, 'trait')]
    pallas_call x0 -> x2, Pallas kernels: none -> 65.7 us  [the longest x1 50.5 us: body(): pl.pallas_call(functools.partial(fit_kernel, n, trait, chunks, min(rows,...]
    dot_general x10 -> x0, matrix products: 33.9 us -> none  [the longest x1 11 us: body(): lax.dot_general(genotype, residual, (((0,), (0,)), ((), ())), preferred_e...]
    all_gather x1 -> x0, blocking collectives: 32.6 us -> none  [body(): targets_full = lax.all_gather(targets, 'snp', axis=0, tiled=True)]
    reduce_sum x4 -> x0, other arithmetic: 28.7 us -> none  [the longest x3 28.6 us: shrink_local(): block_sq = jnp.sum(blocks * blocks, axis=2)]
    mul x1 -> x0, local copies, waits for them, and re-layouts: 17.4 us -> none  [shrink_local(): value = (blocks * block_factor[:, :, None]).reshape(value.shape)]
    unnamed x11 -> x2, local copies, waits for them, and re-layouts: 18.4 us -> 5.71 us
    mul x1 -> x0, other arithmetic: 12 us -> none  [shrink_local(): value = (blocks * block_factor[:, :, None]).reshape(value.shape)]
  transfers between devices with their start and end apart: 5 -> 0, of which waited for: 5 -> 0; matrix products, arithmetic and copies ran while one was open for 6% -> 0% of each run, Pallas kernels for 0% -> 0%
where the time goes in v1:
time: 71.6 us; the launch traced here: 71.5 us
  Pallas kernels  65.7 us (92%)
  local copies, waits for them, and re-layouts  5.71 us (8%)
    pallas_call x1, Pallas kernels, body(): pl.pallas_call(functools.partial(fit_kernel, n, trait, chunks, min(rows,...  50.5 us
    pallas_call x1, Pallas kernels, body(): pl.pallas_call(functools.partial(scale_kernel, pieces, min(rows // pieces...  15.2 us
    unnamed x2, local copies, waits for them, and re-layouts  5.71 us

profile of v1, /device:TPU:0, one launch (start us, length us, event | category | flops | bytes accessed | tf_op | source)
XLA Modules:
  0.0 71.5 jit_solution(5227783050946029437)
XLA Ops:
  0.0 50.5 %fit.1 = (f32[1024,4096]{1,0:T(8,128)S(1)}, f32[1024,128]{1,0:T(8,128)S(1)}) custom-call(bf16[32,1024]{1,0:T(8,128)(2,1)} %g_ref.1, bf16[4,4096]{1,0:T(4,128)(2,1)} %t_ref.1, s32[4,128,128]{2,1,0:T(8,128)} %m_ref.1, f32[4,128]{1,0:T(4,128)} %w_ref.1, f32[1024,4096]{1,0:T(8,128)} %e_hbm.1), custom_call_target="tpu_custom_call" | custom-call | tf_op jit(solution)/shard_map/fit/pallas_call | solution.py:285
  50.5 0.0 copy-start
  50.5 5.7 %copy-done = f32[1024,4096]{1,0:T(8,128)} copy-done((f32[1024,4096]{1,0:T(8,128)}, f32[1024,4096]{1,0:T(8,128)S(1)}, u32[]{:S(2)}) %copy-start) | copy-done | bytes 16777240
  56.2 15.2 %scale.1 = f32[1024,4096]{1,0:T(8,128)} custom-call(f32[1024,4096]{1,0:T(8,128)} %copy-done, f32[1024,128]{1,0:T(8,128)S(1)} %get-tuple-element.8.sc_ref), custom_call_target="tpu_custom_call" | custom-call | tf_op jit(solution)/shard_map/scale/pallas_call | solution.py:320
Async XLA Ops:
  50.5 5.7 %copy-start = (f32[1024,4096]{1,0:T(8,128)}, f32[1024,4096]{1,0:T(8,128)S(1)}, u32[]{:S(2)}) copy-start(f32[1024,4096]{1,0:T(8,128)S(1)} %get-tuple-element.7.v_ref) | copy-start | bytes 50331652

commit v2 on v1

--- a/solution.py
+++ b/solution.py
@@ -12,17 +12,23 @@
 STEP = 0.5
 F32 = jnp.float32
 BF16 = jnp.bfloat16
-WIRE = jnp.float32
+LAG = 2
 MESH = pl.DeviceIdType.MESH
 HIGH = lax.Precision.HIGHEST
 NT = (((1,), (1,)), ((), ()))
 TN = (((0,), (0,)), ((), ()))
 
 
+def aligned(x, m):
+    return x if isinstance(x, int) else pl.multiple_of(x, m)
+
+
 def one_hot_rows(rows, samples, per, half):
     r = lax.broadcasted_iota(jnp.int32, (rows, samples), 0)
     n = lax.broadcasted_iota(jnp.int32, (rows, samples), 1)
-    owner = lax.shift_right_logical(r, 3)
+    slot = lax.shift_right_logical(r, 3)
+    line = rows // SUB // 2
+    owner = jnp.where(slot < line, 2 * slot, 2 * (slot - line) + 1)
     inner = jnp.bitwise_and(r, 7) - half * per
     hit = (n == owner * per + inner) & (inner >= 0) & (inner < per)
     return jnp.where(hit, 1.0, 0.0).astype(BF16)
@@ -32,11 +38,14 @@
     n, trait, chunks, row_tile,
     g_ref, t_ref, m_ref, w_ref, e_hbm,
     v_ref, sc_ref,
-    send, got, res, rg, gs, gt, bq, bt, gq, so, si, ssum, thr,
-    e_sem, rs_send, rs_recv, ag_send, ag_recv, x_send, x_recv, y_send, y_recv,
+    send, near, both, got, res, rg, gs, gt, bq, bt, gq, so, si, ssum, thr,
+    e_sem, p_send, p_recv, rs_send, rs_recv, ag_send, ag_recv, b_send, b_recv, x_send, x_recv, y_send, y_recv,
 ):
     me = lax.axis_index("snp")
     mt = lax.axis_index("trait")
+    mp = lax.rem(me, 2)
+    mz = me // 2
+    nz = n // 2
     samples, rows = g_ref.shape
     per = samples // n
     halves = SUB // per
@@ -48,10 +57,10 @@
     q = rows // trait
 
     def col(h, c):
-        return pl.ds(pl.multiple_of(h * half + c * w, w), w)
+        return pl.ds(aligned(h * half + c * w, w), w)
 
     def part(c):
-        return pl.ds(pl.multiple_of(c * w, w), w)
+        return pl.ds(aligned(c * w, w), w)
 
     def load(h, c):
         return pltpu.make_async_copy(
@@ -64,19 +73,19 @@
 
     barrier = pltpu.get_barrier_semaphore()
 
+    def greet(to):
+        pl.semaphore_signal(barrier, inc=1, device_id=to, device_id_type=MESH)
+
     def greet_snp(k, _):
-        pl.semaphore_signal(
-            barrier, inc=1, device_id={"snp": lax.rem(me + k, n)}, device_id_type=MESH
-        )
+        greet({"snp": 2 * lax.rem(mz + k, nz) + mp})
         return 0
 
     def greet_trait(k, _):
-        pl.semaphore_signal(
-            barrier, inc=1, device_id={"trait": lax.rem(mt + k, trait)}, device_id_type=MESH
-        )
-        return 0
-
-    lax.fori_loop(1, n, greet_snp, 0)
+        greet({"trait": lax.rem(mt + k, trait)})
+        return 0
+
+    greet({"snp": me + 1 - 2 * mp})
+    lax.fori_loop(1, nz, greet_snp, 0)
     lax.fori_loop(1, trait, greet_trait, 0)
 
     for h in range(halves):
@@ -86,25 +95,45 @@
             g_ref[...], pick, (((0,), (1,)), ((), ())), preferred_element_type=F32
         ).astype(BF16)
 
-    pl.semaphore_wait(barrier, n + trait - 2)
+    pl.semaphore_wait(barrier, nz + trait - 1)
+
+    def pair_copy(c):
+        return pltpu.make_async_remote_copy(
+            src_ref=send.at[1 - mp, :, :, part(c)],
+            dst_ref=near.at[:, :, part(c)],
+            send_sem=p_send.at[c],
+            recv_sem=p_recv.at[c],
+            device_id={"snp": me + 1 - 2 * mp},
+            device_id_type=MESH,
+        )
 
     def rs_copy(c, to, frm):
         return pltpu.make_async_remote_copy(
-            src_ref=send.at[to, :, part(c)],
+            src_ref=both.at[to, :, part(c)],
             dst_ref=got.at[frm, :, part(c)],
             send_sem=rs_send.at[c, to],
             recv_sem=rs_recv.at[c, frm],
-            device_id={"snp": to},
+            device_id={"snp": 2 * to + mp},
             device_id_type=MESH,
         )
 
     def ag_copy(c, to, frm):
         return pltpu.make_async_remote_copy(
             src_ref=res.at[:, part(c)],
-            dst_ref=rg.at[frm, :, part(c)],
+            dst_ref=rg.at[mp, frm, :, part(c)],
             send_sem=ag_send.at[c, to],
             recv_sem=ag_recv.at[c, frm],
-            device_id={"snp": to},
+            device_id={"snp": 2 * to + mp},
+            device_id_type=MESH,
+        )
+
+    def back_copy(c, parity):
+        return pltpu.make_async_remote_copy(
+            src_ref=rg.at[parity, :, :, part(c)],
+            dst_ref=rg.at[parity, :, :, part(c)],
+            send_sem=b_send.at[c],
+            recv_sem=b_recv.at[c],
+            device_id={"snp": me + 1 - 2 * mp},
             device_id_type=MESH,
         )
 
@@ -147,12 +176,22 @@
                     v_ref[k * kt : (k + 1) * kt, col(h, c)].astype(BF16),
                     preferred_element_type=F32,
                 )
-        send[:, :, part(c)] = total.reshape(n, SUB, w).astype(send.dtype)
-        got[me, :, part(c)] = send[me, :, part(c)]
-        peers(n, me, lambda p: rs_copy(c, p, me).start())
-        return 0
-
-    lax.fori_loop(0, chunks, fit_chunk, 0)
+        send[:, :, :, part(c)] = total.reshape(2, nz, SUB, w)
+        pair_copy(c).start()
+        return 0
+
+    def pair_chunk(c, _):
+        pair_copy(c).wait_recv()
+        both[:, :, part(c)] = send[mp, :, :, part(c)] + near[:, :, part(c)]
+        peers(nz, mz, lambda p: rs_copy(c, p, mz).start())
+        got[mz, :, part(c)] = both[mz, :, part(c)]
+        return 0
+
+    for c in range(chunks + LAG):
+        if c < chunks:
+            fit_chunk(c, 0)
+        if c >= LAG:
+            pair_chunk(c - LAG, 0)
 
     for level in range(levels):
         member = m_ref[level].astype(F32)
@@ -166,25 +205,26 @@
             member, member, TN, precision=HIGH, preferred_element_type=F32
         )
 
-    def res_chunk(c, _):
-        peers(n, me, lambda p: rs_copy(c, p, p).wait_recv())
-        fitted = jnp.sum(got[:, :, part(c)].astype(F32), axis=0)
+    def res_chunk(c):
+        peers(nz, mz, lambda p: rs_copy(c, p, p).wait_recv())
+        fitted = jnp.sum(got[:, :, part(c)], axis=0)
         target = jnp.concatenate(
             [t_ref[:, col(h, c)].astype(F32) for h in range(halves)], axis=0
         )
         residual = (target - fitted).astype(BF16)
         res[:, part(c)] = residual
-        rg[me, :, part(c)] = residual
-        peers(n, me, lambda p: ag_copy(c, p, me).start())
-        return 0
-
-    lax.fori_loop(0, chunks, res_chunk, 0)
+        rg[mp, mz, :, part(c)] = residual
+        peers(nz, mz, lambda p: ag_copy(c, p, mz).start())
+
+    def back_chunk(c):
+        peers(nz, mz, lambda p: ag_copy(c, p, p).wait_recv())
+        back_copy(c, mp).start()
 
     lane = lax.broadcasted_iota(jnp.int32, (row_tile, TB), 1)
 
     def value_chunk(c, _):
-        peers(n, me, lambda p: ag_copy(c, p, p).wait_recv())
-        resid = rg[:, :, part(c)].reshape(n * SUB, w)
+        back_copy(c, 1 - mp).wait_recv()
+        resid = rg[:, :, :, part(c)].reshape(n * SUB, w)
 
         def tile(i, _):
             r = pl.ds(pl.multiple_of(i * row_tile, row_tile), row_tile)
@@ -205,6 +245,11 @@
         return 0
 
     bq[...] = jnp.zeros_like(bq)
+    for c in range(chunks + 1):
+        if c < chunks:
+            res_chunk(c)
+        if c >= 1:
+            back_chunk(c - 1)
     lax.fori_loop(0, chunks, value_chunk, 0)
 
     for k in range(trait):
@@ -235,8 +280,10 @@
         sc_ref[k * q : (k + 1) * q, :blocks] = si[k].T
 
     def drain(c, _):
-        peers(n, me, lambda p: rs_copy(c, p, me).wait_send())
-        peers(n, me, lambda p: ag_copy(c, p, me).wait_send())
+        pair_copy(c).wait_send()
+        peers(nz, mz, lambda p: rs_copy(c, p, mz).wait_send())
+        peers(nz, mz, lambda p: ag_copy(c, p, mz).wait_send())
+        back_copy(c, mp).wait_send()
         return 0
 
     lax.fori_loop(0, chunks, drain, 0)
@@ -278,21 +325,24 @@
     halves = SUB // (samples // n)
     half = cols // halves
     chunks = 4
+    nz = n // 2
     q = rows // trait
     vmem = pl.BlockSpec(memory_space=pltpu.VMEM)
     hbm = pl.BlockSpec(memory_space=pl.ANY)
     dma = pltpu.SemaphoreType.DMA
     value, scale = pl.pallas_call(
-        functools.partial(fit_kernel, n, trait, chunks, min(rows, 64)),
+        functools.partial(fit_kernel, n, trait, chunks, min(rows, 512)),
         name="fit",
         out_shape=(pltpu.VMEM((rows, cols), F32), pltpu.VMEM((rows, TB), F32)),
         in_specs=[vmem] * 4 + [hbm],
         out_specs=(vmem, vmem),
         scratch_shapes=[
-            pltpu.VMEM((n, SUB, half), WIRE),
-            pltpu.VMEM((n, SUB, half), WIRE),
+            pltpu.VMEM((2, nz, SUB, half), F32),
+            pltpu.VMEM((nz, SUB, half), F32),
+            pltpu.VMEM((nz, SUB, half), F32),
+            pltpu.VMEM((nz, SUB, half), F32),
             pltpu.VMEM((SUB, half), BF16),
-            pltpu.VMEM((n, SUB, half), BF16),
+            pltpu.VMEM((2, nz, SUB, half), BF16),
             pltpu.VMEM((halves, n * SUB, rows), BF16),
             pltpu.VMEM((halves, rows, n * SUB), BF16),
             pltpu.VMEM((rows, TB), F32),
@@ -303,10 +353,14 @@
             pltpu.VMEM((levels, nodes, nodes), F32),
             pltpu.VMEM((levels, nodes, nodes), F32),
             dma((chunks, halves)),
-            dma((chunks, n)),
-            dma((chunks, n)),
-            dma((chunks, n)),
-            dma((chunks, n)),
+            dma((chunks,)),
+            dma((chunks,)),
+            dma((chunks, nz)),
+            dma((chunks, nz)),
+            dma((chunks, nz)),
+            dma((chunks, nz)),
+            dma((chunks,)),
+            dma((chunks,)),
             dma((trait,)),
             dma((trait,)),
             dma((trait,)),
@@ -316,9 +370,11 @@
             collective_id=0, has_side_effects=True, vmem_limit_bytes=40 << 20
         ),
     )(genotype, targets, membership, node_weight, effect_sizes)
+    value = pltpu.with_memory_space_constraint(value, pltpu.VMEM)
+    scale = pltpu.with_memory_space_constraint(scale, pltpu.VMEM)
     pieces = 8
     return pl.pallas_call(
-        functools.partial(scale_kernel, pieces, min(rows // pieces, 32)),
+        functools.partial(scale_kernel, pieces, min(rows // pieces, 128)),
         name="scale",
         out_shape=jax.ShapeDtypeStruct((rows, cols), F32),
         in_specs=[vmem, vmem],

time: 71.6 us -> 45.2 us (0.63)
  Pallas kernels: 65.7 us -> 45.1 us
  local copies, waits for them, and re-layouts: 5.71 us -> 0 us
    pallas_call x1, Pallas kernels: 50.5 us -> 38.5 us  [body(): pl.pallas_call(functools.partial(fit_kernel, n, trait, chunks, min(rows,...]
    pallas_call x1, Pallas kernels: 15.2 us -> 6.64 us  [body(): pl.pallas_call(functools.partial(scale_kernel, pieces, min(rows // pieces...]
    unnamed x2 -> x0, local copies, waits for them, and re-layouts: 5.71 us -> none
where the time goes in v2:
time: 45.2 us; the launch traced here: 45.1 us
  Pallas kernels  45.1 us (100%)
    pallas_call x1, Pallas kernels, body(): pl.pallas_call(functools.partial(fit_kernel, n, trait, chunks, min(rows,...  38.5 us
    pallas_call x1, Pallas kernels, body(): pl.pallas_call(functools.partial(scale_kernel, pieces, min(rows // pieces...  6.64 us

profile of v2, /device:TPU:0, one launch (start us, length us, event | category | flops | bytes accessed | tf_op | source)
XLA Modules:
  0.0 45.1 jit_solution(15904098958681463917)
XLA Ops:
  0.0 38.5 %fit.1 = (f32[1024,4096]{1,0:T(8,128)S(1)}, f32[1024,128]{1,0:T(8,128)S(1)}) custom-call(bf16[32,1024]{1,0:T(8,128)(2,1)} %g_ref.1, bf16[4,4096]{1,0:T(4,128)(2,1)} %t_ref.1, s32[4,128,128]{2,1,0:T(8,128)} %m_ref.1, f32[4,128]{1,0:T(4,128)} %w_ref.1, f32[1024,4096]{1,0:T(8,128)} %e_hbm.1), custom_call_target="tpu_custom_call" | custom-call | tf_op jit(solution)/shard_map/fit/pallas_call | solution.py:333
  38.5 6.6 %scale.1 = f32[1024,4096]{1,0:T(8,128)} custom-call(f32[1024,4096]{1,0:T(8,128)S(1)} %get-tuple-element.7.v_ref, f32[1024,128]{1,0:T(8,128)S(1)} %get-tuple-element.8.sc_ref), custom_call_target="tpu_custom_call" | custom-call | tf_op jit(solution)/shard_map/scale/pallas_call | solution.py:376

commit v3 on v2

--- a/solution.py
+++ b/solution.py
@@ -95,6 +95,18 @@
             g_ref[...], pick, (((0,), (1,)), ((), ())), preferred_element_type=F32
         ).astype(BF16)
 
+    for level in range(levels):
+        member = m_ref[level].astype(F32)
+        count = jnp.sum(member, axis=1, keepdims=True)
+        weight = jnp.broadcast_to(w_ref[level : level + 1, :], member.shape).T
+        by_node = STEP * weight * jnp.sqrt(TB * jnp.maximum(count, 1.0))
+        thr[level] = lax.dot_general(
+            member, by_node, TN, precision=HIGH, preferred_element_type=F32
+        )
+        ssum[level] = lax.dot_general(
+            member, member, TN, precision=HIGH, preferred_element_type=F32
+        )
+
     pl.semaphore_wait(barrier, nz + trait - 1)
 
     def pair_copy(c):
@@ -192,18 +204,6 @@
             fit_chunk(c, 0)
         if c >= LAG:
             pair_chunk(c - LAG, 0)
-
-    for level in range(levels):
-        member = m_ref[level].astype(F32)
-        count = jnp.sum(member, axis=1, keepdims=True)
-        weight = jnp.broadcast_to(w_ref[level : level + 1, :], member.shape).T
-        by_node = STEP * weight * jnp.sqrt(TB * jnp.maximum(count, 1.0))
-        thr[level] = lax.dot_general(
-            member, by_node, TN, precision=HIGH, preferred_element_type=F32
-        )
-        ssum[level] = lax.dot_general(
-            member, member, TN, precision=HIGH, preferred_element_type=F32
-        )
 
     def res_chunk(c):
         peers(nz, mz, lambda p: rs_copy(c, p, p).wait_recv())

time: 45.2 us -> 45.2 us (level)
  no operation moved by 1% of the time
where the time goes in v3:
time: 45.2 us; the launch traced here: 45.1 us
  Pallas kernels  45.1 us (100%)
    pallas_call x1, Pallas kernels, body(): pl.pallas_call(functools.partial(fit_kernel, n, trait, chunks, min(rows,...  38.4 us
    pallas_call x1, Pallas kernels, body(): pl.pallas_call(functools.partial(scale_kernel, pieces, min(rows // pieces...  6.64 us

profile of v3, /device:TPU:0, one launch (start us, length us, event | category | flops | bytes accessed | tf_op | source)
XLA Modules:
  0.0 45.1 jit_solution(16593324184334142922)
XLA Ops:
  0.0 38.4 %fit.1 = (f32[1024,4096]{1,0:T(8,128)S(1)}, f32[1024,128]{1,0:T(8,128)S(1)}) custom-call(bf16[32,1024]{1,0:T(8,128)(2,1)} %g_ref.1, bf16[4,4096]{1,0:T(4,128)(2,1)} %t_ref.1, s32[4,128,128]{2,1,0:T(8,128)} %m_ref.1, f32[4,128]{1,0:T(4,128)} %w_ref.1, f32[1024,4096]{1,0:T(8,128)} %e_hbm.1), custom_call_target="tpu_custom_call" | custom-call | tf_op jit(solution)/shard_map/fit/pallas_call | solution.py:333
  38.5 6.6 %scale.1 = f32[1024,4096]{1,0:T(8,128)} custom-call(f32[1024,4096]{1,0:T(8,128)S(1)} %get-tuple-element.7.v_ref, f32[1024,128]{1,0:T(8,128)S(1)} %get-tuple-element.8.sc_ref), custom_call_target="tpu_custom_call" | custom-call | tf_op jit(solution)/shard_map/scale/pallas_call | solution.py:376
